TPU v7x, 512 devices: a whole 4x4x16 slice. The times are simulated.
512 devices in a mesh: dp: 32 (over x, y, core), expert: 16 (over z).
Axes of the slice: x: 4, y: 4, z: 16, core: 2. Of those that a mesh axis runs over, the one named last changes fastest.
Arguments:
- tokens: bfloat16 [65536, 2048], P(('dp', 'expert')), may hold values from -200 to 200
- norm_gain: float32 [2048], replicated, may hold values from 0.1 to 1.9
- route_probs: float32 [65536, 8], P(('dp', 'expert')), may hold values from 0.02 to 4
- window_expert: int32 [65536], P(('dp', 'expert')), may hold values from 0 to 15, as said below
- w_gate_up: bfloat16 [16, 768, 4096], P('expert', 'dp'), may hold values from -0.125 to 0.125
- w_down: bfloat16 [16, 2048, 768], P('expert', 'dp'), may hold values from -0.21875 to 0.21875
Outputs:
- moe_out: bfloat16 [65536, 2048], P(('dp', 'expert'))
Inputs may be any that keep to these rules, and one draw needn't show every extreme that they name: `window_expert`: in the tokens of one device no expert is named by more than 24 tokens; one expert, the same for every device, is named by exactly 24 tokens of every device.
All inputs are finite; a program needn't handle non-finite values.
Results may differ from a plain program's by a relative error of at most 0.0071.
Values may be sent and summed in bfloat16 or wider, within the bound.
No kernel may reach another device: no remote copies, remote signals or barrier semaphores. Data moves between devices by JAX's collectives and lax.ppermute only.
A program may use at most 64 MiB of HBM per device.

v0:
```python
import jax
import jax.numpy as jnp
from jax import lax
from jax.sharding import PartitionSpec as P


def send_rows(outgoing):
    return lax.all_to_all(outgoing, "expert", split_axis=0, concat_axis=0, tiled=True)


def local(tokens, norm_gain, route_probs, window_expert, w_gate_up, w_down):
    tok_count = tokens.shape[0]
    width = tokens.shape[1]
    owners = lax.axis_size("expert")
    capacity = 3 * tok_count // owners
    values = tokens.astype(jnp.float32)
    meansq = jnp.mean(values * values, axis=1, keepdims=True)
    normed = (values * lax.rsqrt(meansq + 1e-06) * norm_gain[None, :]).astype(jnp.bfloat16)
    share = route_probs[:, 0] / jnp.sum(route_probs, axis=1)
    member = (window_expert[:, None] == jnp.arange(owners, dtype=jnp.int32)[None, :]).astype(
        jnp.int32
    )
    earlier = jnp.cumsum(member, axis=0) - member
    slot_index = jnp.sum(earlier * member, axis=1)
    place = window_expert * capacity + slot_index
    source = (
        jnp.full((owners * capacity,), tok_count, jnp.int32)
        .at[place]
        .set(jnp.arange(tok_count, dtype=jnp.int32))
    )
    outgoing = jnp.take(normed, source, axis=0, mode="fill", fill_value=0).reshape(
        owners, capacity, width
    )
    local_both = w_gate_up[0]
    contract = (((1,), (1,)), ((), ()))
    arrived = send_rows(outgoing).reshape(owners * capacity, width)
    piece = lax.all_gather(local_both, "dp", axis=0, tiled=True)
    gate = lax.dot_general(arrived, piece[:, :width], contract, preferred_element_type=jnp.float32)
    upper = lax.dot_general(arrived, piece[:, width:], contract, preferred_element_type=jnp.float32)
    hidden = (jax.nn.silu(gate) * upper).astype(jnp.bfloat16)
    produced = lax.dot_general(
        hidden,
        lax.all_gather(w_down[0], "dp", axis=0, tiled=True),
        contract,
        preferred_element_type=jnp.float32,
    ).astype(jnp.bfloat16)
    returned = lax.all_to_all(
        produced.reshape(owners, capacity, width), "expert", split_axis=0, concat_axis=0, tiled=True
    )
    returned = returned.reshape(owners * capacity, width)
    picked = jnp.take(returned, place, axis=0).astype(jnp.float32)
    return (share[:, None] * picked).astype(jnp.bfloat16)


def solution(mesh):
    placed = (
        P(("dp", "expert"), None),
        P(),
        P(("dp", "expert"), None),
        P(("dp", "expert")),
        P("expert", "dp", None),
        P("expert", "dp", None),
    )
    return jax.shard_map(
        local, mesh=mesh, in_specs=placed, out_specs=P(("dp", "expert"), None), check_vma=False
    )
```

profile of v0, /device:TPU:24, one launch (start us, length us, event | category | flops | bytes accessed | tf_op | source)
XLA Modules:
  0.0 244.4 jit_solution(1626196605800188457)
XLA Ops:
  6.5 0.0 all-gather.5.cloned.1.call-start
  6.5 0.7 all-gather.5.cloned.1.call-update
  7.3 0.7 fusion.21
  8.0 0.2 reduce_window_sum.11
  8.2 0.8 select_reduce_fusion
  9.0 0.7 compare_and_fusion.1
  9.7 1.0 scatter_custom_fusion
  10.7 0.1 broadcast_in_dim.38
  10.8 1.2 fusion.15
  12.0 1.2 fusion.17
  13.3 2.5 %gather_fusion = bf16[384,2048]{1,0:T(8,128)(2,1)S(1)} fusion(bf16[128,2048]{1,0:T(8,128)(2,1)S(1)} %fusion.17, s32[1024]{0:T(1024)S(1)} %pad_clamp_fusion.1), kind=kCustom, calls=%fused_computation | custom fusion | bytes 3147264 | tf_op jit(solution)/shard_map/jit(_take)/gather | solution.py:31
  15.7 1.3 broadcast_select_fusion
  17.1 15.2 %all-to-all-start = ((bf16[16,24,2048]{2,1,0:T(8,128)(2,1)}), bf16[16,24,2048]{2,1,0:T(8,128)(2,1)S(1)}, u32[]{:S(2)}, u32[]{:S(2)}) async-start(bf16[16,24,2048]{2,1,0:T(8,128)(2,1)} %broadcast_select_fusion), calls=%async_computation | async-start | bytes 3145728 | tf_op jit(solution)/shard_map/all_to_all | solution.py:8
  32.3 0.0 all-gather.7.cloned.1.call-start
  32.3 0.7 all-gather.7.cloned.1.call-update
  33.0 73.5 %all-to-all-done = bf16[16,24,2048]{2,1,0:T(8,128)(2,1)S(1)} async-done(((bf16[16,24,2048]{2,1,0:T(8,128)(2,1)}), bf16[16,24,2048]{2,1,0:T(8,128)(2,1)S(1)}, u32[]{:S(2)}, u32[]{:S(2)}) %all-to-all-start) | async-done | bytes 1572896 | tf_op jit(solution)/shard_map/all_to_all | solution.py:8
  106.6 0.0 all-gather.5.cloned.1.call-done
  106.6 3.3 %fusion.2 = f32[384,768]{1,0:T(8,128)S(1)} fusion(bf16[384,2048]{1,0:T(8,128)(2,1)S(1)} %bitcast.20, bf16[768,4096]{1,0:T(8,128)(2,1)} %bitcast.22), kind=kOutput, calls=%fused_computation.5 | convolution fusion | flops 1207959552 | bytes 5898240 | tf_op jit(solution)/shard_map/dot_general | solution.py:38
  109.9 31.4 %all-gather.7.cloned.1.call-done = bf16[1,2048,768]{2,1,0:T(8,128)(2,1)} async-done(((bf16[1,64,768]{2,1,0:T(8,128)(2,1)}), bf16[1,2048,768]{2,1,0:T(8,128)(2,1)}) %all-gather.7.cloned.1.call-update) | async-done | bytes 3145744 | tf_op jit(solution)/shard_map/all_gather | solution.py:43
  141.3 7.1 %fusion.6 = bf16[384,2048]{1,0:T(8,128)(2,1)} fusion(bf16[1,2048,768]{2,1,0:T(8,128)(2,1)} %all-gather.7.cloned.1.call-done, bf16[384,2048]{1,0:T(8,128)(2,1)S(1)} %bitcast.21, bf16[768,4096]{1,0:T(8,128)(2,1)} %bitcast.23, f32[384,768]{1,0:T(8,128)S(1)} %fusion.2), kind=kOutput, calls=%fused_computation.9 | convolution fusion | flops 2418475008 | bytes 10616832 | tf_op jit(solution)/shard_map/dot_general | solution.py:41
  148.5 0.0 copy-start
  148.5 12.4 %all-to-all-start.1 = ((bf16[16,24,2048]{2,1,0:T(8,128)(2,1)}), bf16[16,24,2048]{2,1,0:T(8,128)(2,1)S(1)}, u32[]{:S(2)}, u32[]{:S(2)}) async-start(bf16[16,24,2048]{2,1,0:T(8,128)(2,1)} %bitcast.6), calls=%async_computation.1 | async-start | bytes 3145728 | tf_op jit(solution)/shard_map/all_to_all | solution.py:47
  160.9 0.0 copy-done
  161.0 74.5 %all-to-all-done.1 = bf16[16,24,2048]{2,1,0:T(8,128)(2,1)S(1)} async-done(((bf16[16,24,2048]{2,1,0:T(8,128)(2,1)}), bf16[16,24,2048]{2,1,0:T(8,128)(2,1)S(1)}, u32[]{:S(2)}, u32[]{:S(2)}) %all-to-all-start.1) | async-done | bytes 1572896 | tf_op jit(solution)/shard_map/all_to_all | solution.py:47
  235.5 0.9 gather_fusion.1
  236.4 1.1 multiply_convert_fusion
  (8 shorter events, 0.1 us)
Async XLA Ops:
  6.5 100.0 %all-gather.5.cloned.1.call-start = ((), (), s32[]{:S(2)}) async-start(), calls=%async_computation.2 | async-start | bytes 6488064 | tf_op jit(solution)/shard_map/all_gather | solution.py:37
  17.1 89.5 %all-to-all-start = ((bf16[16,24,2048]{2,1,0:T(8,128)(2,1)}), bf16[16,24,2048]{2,1,0:T(8,128)(2,1)S(1)}, u32[]{:S(2)}, u32[]{:S(2)}) async-start(bf16[16,24,2048]{2,1,0:T(8,128)(2,1)} %broadcast_select_fusion), calls=%async_computation | async-start | bytes 3145728 | tf_op jit(solution)/shard_map/all_to_all | solution.py:8
  32.3 109.1 %all-gather.7.cloned.1.call-start = ((), (), s32[]{:S(2)}) async-start(), calls=%async_computation.3 | async-start | bytes 3244032 | tf_op jit(solution)/shard_map/all_gather | solution.py:43
  148.5 12.4 %copy-start = (f32[128,8]{0,1:T(8,128)S(1)}, f32[128,8]{0,1:T(8,128)}, u32[]{:S(2)}) copy-start(f32[128,8]{0,1:T(8,128)} %param.8) | copy-start | bytes 12292
  148.5 87.0 %all-to-all-start.1 = ((bf16[16,24,2048]{2,1,0:T(8,128)(2,1)}), bf16[16,24,2048]{2,1,0:T(8,128)(2,1)S(1)}, u32[]{:S(2)}, u32[]{:S(2)}) async-start(bf16[16,24,2048]{2,1,0:T(8,128)(2,1)} %bitcast.6), calls=%async_computation.1 | async-start | bytes 3145728 | tf_op jit(solution)/shard_map/all_to_all | solution.py:47
Sparse Core Ops, SparseCore 0:
  10.5 67.8 all-gather.4
  81.5 59.8 all-gather.6
where the time goes:
time: 245 us; the launch traced here: 244 us
  waiting for transfers between devices  181 us (74%)
  starting transfers between devices  27.7 us (11%)
  between operations  13.5 us (6%)
  matrix products  10.5 us (4%)
  other arithmetic  7.39 us (3%)
  local copies, waits for them, and re-layouts  4.46 us (2%)
    all_to_all x1, waiting for transfers between devices, local(): lax.all_to_all(produced.reshape(owners, capacity, width), 'expert', split...  74.5 us
    all_to_all x1, waiting for transfers between devices, send_rows(): lax.all_to_all(outgoing, 'expert', split_axis=0, concat_axis=0, tiled=True)  73.5 us
    all_gather x1, waiting for transfers between devices, local(): lax.all_gather(w_down[0], 'dp', axis=0, tiled=True)  31.4 us
    all_to_all x1, starting transfers between devices, send_rows(): lax.all_to_all(outgoing, 'expert', split_axis=0, concat_axis=0, tiled=True)  15.2 us
    all_to_all x1, starting transfers between devices, local(): lax.all_to_all(produced.reshape(owners, capacity, width), 'expert', split...  12.4 us
    dot_general x1, matrix products, local(): lax.dot_general(hidden, lax.all_gather(w_down[0], 'dp', axis=0, tiled=Tru...  7.14 us
  transfers between devices with their start and end apart: 4, of which 3 were waited for; matrix products, arithmetic and copies ran while one was open for 5% of the time, Pallas kernels for 0%

commit v1 on v0

--- a/solution.py
+++ b/solution.py
@@ -6,6 +6,25 @@
 
 def send_rows(outgoing):
     return lax.all_to_all(outgoing, "expert", split_axis=0, concat_axis=0, tiled=True)
+
+
+def pack(both, down):
+    corner = jnp.concatenate([down[48:56, 512:], down[56:64, 512:]], axis=1)
+    tail = jnp.concatenate([down[48:64, :512], corner], axis=0)
+    return jnp.concatenate([both, down[:24], down[24:48], tail], axis=1)
+
+
+def unpack_down(gathered, width):
+    rows = gathered[:, 2 * width :].reshape(-1, 24, width)
+    third = jnp.concatenate(
+        [
+            rows[:, :16, 1536:],
+            jnp.concatenate([rows[:, 16:, 1536:1792], rows[:, 16:, 1792:]], axis=1),
+        ],
+        axis=2,
+    )
+    down = jnp.concatenate([rows[:, :, :768], rows[:, :, 768:1536], third], axis=1)
+    return down.reshape(width, 768)
 
 
 def local(tokens, norm_gain, route_probs, window_expert, w_gate_up, w_down):
@@ -31,16 +50,16 @@
     outgoing = jnp.take(normed, source, axis=0, mode="fill", fill_value=0).reshape(
         owners, capacity, width
     )
-    local_both = w_gate_up[0]
+    piece = lax.all_gather(pack(w_gate_up[0], w_down[0]), "dp", axis=0, tiled=True)
+    down = unpack_down(piece, width)
     contract = (((1,), (1,)), ((), ()))
     arrived = send_rows(outgoing).reshape(owners * capacity, width)
-    piece = lax.all_gather(local_both, "dp", axis=0, tiled=True)
     gate = lax.dot_general(arrived, piece[:, :width], contract, preferred_element_type=jnp.float32)
-    upper = lax.dot_general(arrived, piece[:, width:], contract, preferred_element_type=jnp.float32)
+    upper = lax.dot_general(arrived, piece[:, width : 2 * width], contract, preferred_element_type=jnp.float32)
     hidden = (jax.nn.silu(gate) * upper).astype(jnp.bfloat16)
     produced = lax.dot_general(
         hidden,
-        lax.all_gather(w_down[0], "dp", axis=0, tiled=True),
+        down,
         contract,
         preferred_element_type=jnp.float32,
     ).astype(jnp.bfloat16)

time: 245 us -> 210 us (0.86)
  waiting for transfers between devices: 181 us -> 146 us
  starting transfers between devices: 27.7 us -> 21.4 us
  local copies, waits for them, and re-layouts: 4.46 us -> 9.28 us
    all_to_all x1, waiting for transfers between devices: 73.5 us -> 19.6 us  [send_rows(): lax.all_to_all(outgoing, 'expert', split_axis=0, concat_axis=0, tiled=True)]
    all_gather x2 -> x1, waiting for transfers between devices: 31.4 us -> 51.8 us  [local(): lax.all_gather(pack(w_gate_up[0], w_down[0]), 'dp', axis=0, tiled=True)]
    all_to_all x1, starting transfers between devices: 12.4 us -> 6.17 us  [local(): lax.all_to_all(produced.reshape(owners, capacity, width), 'expert', split...]
    slice x0 -> x7, local copies, waits for them, and re-layouts: none -> 4.81 us  [the longest x1 2.29 us: unpack_down(): rows = gathered[:, 2 * width:].reshape(-1, 24, width)]
  transfers between devices with their start and end apart: 4 -> 3, of which waited for: 3 -> 3; matrix products, arithmetic and copies ran while one was open for 5% -> 5% of each run, Pallas kernels for 0% -> 0%
where the time goes in v1:
time: 210 us; the launch traced here: 209 us
  waiting for transfers between devices  146 us (70%)
  starting transfers between devices  21.4 us (10%)
  between operations  13.6 us (6%)
  matrix products  11.8 us (6%)
  local copies, waits for them, and re-layouts  9.28 us (4%)
  other arithmetic  7.27 us (3%)
    all_to_all x1, waiting for transfers between devices, local(): lax.all_to_all(produced.reshape(owners, capacity, width), 'expert', split...  74.4 us
    all_gather x1, waiting for transfers between devices, local(): lax.all_gather(pack(w_gate_up[0], w_down[0]), 'dp', axis=0, tiled=True)  51.8 us
    all_to_all x1, waiting for transfers between devices, send_rows(): lax.all_to_all(outgoing, 'expert', split_axis=0, concat_axis=0, tiled=True)  19.6 us
    all_to_all x1, starting transfers between devices, send_rows(): lax.all_to_all(outgoing, 'expert', split_axis=0, concat_axis=0, tiled=True)  15.2 us
    dot_general x1, matrix products, local(): lax.dot_general(hidden, down, contract, preferred_element_type=jnp.float32)  6.94 us
    all_to_all x1, starting transfers between devices, local(): lax.all_to_all(produced.reshape(owners, capacity, width), 'expert', split...  6.17 us
    dot_general x1, matrix products, local(): lax.dot_general(arrived, piece[:, :width], contract, preferred_element_ty...  4.87 us
  transfers between devices with their start and end apart: 3, of which 3 were waited for; matrix products, arithmetic and copies ran while one was open for 5% of the time, Pallas kernels for 0%

profile of v1, /device:TPU:24, one launch (start us, length us, event | category | flops | bytes accessed | tf_op | source)
XLA Modules:
  0.0 209.2 jit_solution(5654556108240286351)
XLA Ops:
  6.5 0.0 copy-start
  6.5 0.0 copy-start.1
  6.5 0.0 all-gather.2.cloned.1.call-start
  6.5 0.8 slice_bitcast_fusion.1
  7.4 0.7 fusion.23
  8.1 0.7 slice.68
  8.8 1.7 maximum_maximum_fusion.1
  10.5 0.0 all-gather.2.cloned.1.call-update
  10.5 0.7 fusion.16
  11.2 0.2 reduce_window_sum.11
  11.4 0.8 select_reduce_fusion
  12.2 0.7 compare_and_fusion.1
  12.9 1.0 scatter_custom_fusion
  13.9 0.1 broadcast_in_dim.38
  14.0 0.0 copy-done
  14.1 0.2 fusion.10
  14.2 0.0 copy-done.1
  14.3 0.2 fusion.12
  14.5 2.5 %gather_fusion = bf16[384,2048]{1,0:T(8,128)(2,1)S(1)} fusion(bf16[128,2048]{1,0:T(8,128)(2,1)S(1)} %fusion.12, s32[1024]{0:T(1024)S(1)} %pad_clamp_fusion.1), kind=kCustom, calls=%fused_computation | custom fusion | bytes 3147264 | tf_op jit(solution)/shard_map/jit(_take)/gather | solution.py:50
  16.9 1.3 broadcast_select_fusion
  18.2 15.2 %all-to-all-start = ((bf16[16,24,2048]{2,1,0:T(8,128)(2,1)}), bf16[16,24,2048]{2,1,0:T(8,128)(2,1)}, u32[]{:S(2)}, u32[]{:S(2)}) async-start(bf16[16,24,2048]{2,1,0:T(8,128)(2,1)} %broadcast_select_fusion), calls=%async_computation | async-start | bytes 3145728 | tf_op jit(solution)/shard_map/all_to_all | solution.py:8
  33.5 51.8 %all-gather.2.cloned.1.call-done = bf16[768,6144]{1,0:T(8,128)(2,1)} async-done(((bf16[24,6144]{1,0:T(8,128)(2,1)}), bf16[768,6144]{1,0:T(8,128)(2,1)}) %all-gather.2.cloned.1.call-update) | async-done | bytes 9437200 | tf_op jit(solution)/shard_map/all_gather | solution.py:53
  85.3 2.3 %slice.73 = bf16[768,2048]{1,0:T(8,128)(2,1)S(1)} slice(bf16[768,6144]{1,0:T(8,128)(2,1)} %all-gather.2.cloned.1.call-done), slice={[0:768], [4096:6144]} | slice | bytes 6291456 | tf_op jit(solution)/shard_map/slice | solution.py:18
  87.6 0.2 fusion.21
  87.8 0.3 maximum_maximum_fusion
  88.2 19.6 %all-to-all-done = bf16[16,24,2048]{2,1,0:T(8,128)(2,1)} async-done(((bf16[16,24,2048]{2,1,0:T(8,128)(2,1)}), bf16[16,24,2048]{2,1,0:T(8,128)(2,1)}, u32[]{:S(2)}, u32[]{:S(2)}) %all-to-all-start) | async-done | bytes 1572896 | tf_op jit(solution)/shard_map/all_to_all | solution.py:8
  107.8 4.9 %fusion.2 = f32[384,768]{1,0:T(8,128)} fusion(bf16[384,2048]{1,0:T(8,128)(2,1)} %bitcast.3, bf16[768,6144]{1,0:T(8,128)(2,1)} %all-gather.2.cloned.1.call-done), kind=kOutput, calls=%fused_computation.5 | convolution fusion | flops 1207959552 | bytes 5898240 | tf_op jit(solution)/shard_map/dot_general | solution.py:57
  112.7 6.9 %convolution_convert_fusion = bf16[384,2048]{1,0:T(8,128)(2,1)} fusion(bf16[2048,768]{1,0:T(8,128)(2,1)S(1)} %bitcast.26, bf16[384,2048]{1,0:T(8,128)(2,1)} %bitcast.3, bf16[768,6144]{1,0:T(8,128)(2,1)} %all-gather.2.cloned.1.call-done, f32[384,768]{1,0:T(8,128)} %fusion.2), kind=kOutput, calls=%fused_computation.8 | convolution fusion | flops 2418475008 | bytes 10616832 | tf_op jit(solution)/shard_map/dot_general | solution.py:60
  119.6 0.0 copy-start.2
  119.6 6.2 %all-to-all-start.1 = ((bf16[16,24,2048]{2,1,0:T(8,128)(2,1)}), bf16[16,24,2048]{2,1,0:T(8,128)(2,1)S(1)}, u32[]{:S(2)}, u32[]{:S(2)}) async-start(bf16[16,24,2048]{2,1,0:T(8,128)(2,1)} %bitcast.27), calls=%async_computation.1 | async-start | bytes 3145728 | tf_op jit(solution)/shard_map/all_to_all | solution.py:66
  125.8 0.0 copy-done.2
  125.9 74.4 %all-to-all-done.1 = bf16[16,24,2048]{2,1,0:T(8,128)(2,1)S(1)} async-done(((bf16[16,24,2048]{2,1,0:T(8,128)(2,1)}), bf16[16,24,2048]{2,1,0:T(8,128)(2,1)S(1)}, u32[]{:S(2)}, u32[]{:S(2)}) %all-to-all-start.1) | async-done | bytes 1572896 | tf_op jit(solution)/shard_map/all_to_all | solution.py:66
  200.3 0.9 gather_fusion.1
  201.3 1.1 multiply_convert_fusion
  (10 shorter events, 0.1 us)
Async XLA Ops:
  6.5 7.5 %copy-start = (bf16[128,2048]{1,0:T(8,128)(2,1)S(1)}, bf16[128,2048]{1,0:T(8,128)(2,1)}, u32[]{:S(2)}) copy-start(bf16[128,2048]{1,0:T(8,128)(2,1)} %param.6) | copy-start | bytes 1572868
  6.5 7.7 %copy-start.1 = (f32[2048]{0:T(1024)S(1)}, f32[2048]{0:T(1024)}, u32[]{:S(2)}) copy-start(f32[2048]{0:T(1024)} %param.7) | copy-start | bytes 24580
  6.5 78.7 %all-gather.2.cloned.1.call-start = ((), (), s32[]{:S(2)}) async-start(), calls=%async_computation.2 | async-start | bytes 9732096 | tf_op jit(solution)/shard_map/all_gather | solution.py:53
  18.2 89.6 %all-to-all-start = ((bf16[16,24,2048]{2,1,0:T(8,128)(2,1)}), bf16[16,24,2048]{2,1,0:T(8,128)(2,1)}, u32[]{:S(2)}, u32[]{:S(2)}) async-start(bf16[16,24,2048]{2,1,0:T(8,128)(2,1)} %broadcast_select_fusion), calls=%async_computation | async-start | bytes 3145728 | tf_op jit(solution)/shard_map/all_to_all | solution.py:8
  119.6 6.2 %copy-start.2 = (f32[128,8]{0,1:T(8,128)S(1)}, f32[128,8]{0,1:T(8,128)}, u32[]{:S(2)}) copy-start(f32[128,8]{0,1:T(8,128)} %param.8) | copy-start | bytes 12292
  119.6 80.7 %all-to-all-start.1 = ((bf16[16,24,2048]{2,1,0:T(8,128)(2,1)}), bf16[16,24,2048]{2,1,0:T(8,128)(2,1)S(1)}, u32[]{:S(2)}, u32[]{:S(2)}) async-start(bf16[16,24,2048]{2,1,0:T(8,128)(2,1)} %bitcast.27), calls=%async_computation.1 | async-start | bytes 3145728 | tf_op jit(solution)/shard_map/all_to_all | solution.py:66
Sparse Core Ops, SparseCore 0:
  10.6 74.6 all-gather.1

commit v2 on v0

v2 whole, which is shorter than its diff:
```python
import functools

import jax
import jax.numpy as jnp
from jax import lax
from jax.experimental import pallas as pl
from jax.experimental.pallas import tpu as pltpu
from jax.sharding import PartitionSpec as P

F32, BF16 = jnp.float32, jnp.bfloat16
NT = (((1,), (1,)), ((), ()))
NN = (((1,), (0,)), ((), ()))
VMEM = pl.BlockSpec(memory_space=pltpu.VMEM)
HBM = pl.BlockSpec(memory_space=pltpu.HBM)
ANY = pl.BlockSpec(memory_space=pl.ANY)


def trade(x, mask):
    return lax.ppermute(x, "dp", [(i, i ^ mask) for i in range(lax.axis_size("dp"))])


X_STEPS, Y_STEPS, CORE = (8, 24), (2, 6), 1


def gather(x, steps):
    for mask in steps[:-1]:
        x = jnp.concatenate([x, trade(x, mask)], axis=0)
    y = trade(x, steps[-1])
    return x, y, trade(x, CORE), trade(y, CORE)


def gray(k):
    return k ^ (k >> 1)


def place_mask(slot, x_first):
    low, high = gray(slot & 3), gray((slot >> 2) & 3)
    px, py = (low, high) if x_first else (high, low)
    return (px << 3) | (py << 1) | (slot >> 4)


def send_kernel(tok_ref, gain_ref, expert_ref, out_ref, *, ring, cap):
    values = tok_ref[...].astype(F32)
    meansq = jnp.mean(values * values, axis=1, keepdims=True)
    normed = (values * lax.rsqrt(meansq + 1e-06) * gain_ref[...]).astype(BF16)
    expert = expert_ref[...]
    count = expert.shape[1]
    member = lax.broadcasted_iota(jnp.int32, (ring, count), 0) == expert
    before = lax.broadcasted_iota(jnp.int32, (count, count), 0) < lax.broadcasted_iota(
        jnp.int32, (count, count), 1
    )
    earlier = lax.dot_general(
        member.astype(F32), before.astype(F32), NN, preferred_element_type=F32
    )
    slot = jnp.sum(jnp.where(member, earlier, 0.0), axis=0, keepdims=True).astype(jnp.int32)
    place = expert * cap + slot
    pick = lax.broadcasted_iota(jnp.int32, (ring * cap, count), 0) == place
    out_ref[...] = lax.dot_general(
        pick.astype(F32).astype(BF16), normed, NN, preferred_element_type=F32
    ).astype(BF16)


def arrange_kernel(*refs):
    pieces_a, pieces_b, (up, down, sem_a, sem_b) = refs[:4], refs[4:8], refs[8:]
    me = lax.axis_index("dp")
    each = pieces_a[0].shape[0]
    copies = []
    for q in range(4):
        for p in range(each):
            slot = each * q + p
            for pieces, whole, sem, x_first in (
                (pieces_a, up, sem_a, True),
                (pieces_b, down, sem_b, False),
            ):
                copies.append(
                    pltpu.make_async_copy(
                        pieces[q].at[p], whole.at[me ^ place_mask(slot, x_first)], sem.at[slot]
                    )
                )
    for copy in copies:
        copy.start()
    for copy in copies:
        copy.wait()


def arrange(pieces_a, pieces_b):
    shapes = [(4 * ps[0].shape[0],) + ps[0].shape[1:] for ps in (pieces_a, pieces_b)]
    return pl.pallas_call(
        arrange_kernel,
        out_shape=[jax.ShapeDtypeStruct(shape, BF16) for shape in shapes],
        in_specs=[ANY] * 8,
        out_specs=[HBM] * 2,
        scratch_shapes=[pltpu.SemaphoreType.DMA((shapes[0][0],))] * 2,
        cost_estimate=pl.CostEstimate(flops=0, bytes_accessed=38 << 19, transcendentals=0),
        name="arrange",
    )(*pieces_a, *pieces_b)


def expert_kernel(x_ref, up_hbm, down_hbm, out_ref, up_ref, down_ref, hid, sem_up, sem_down):
    width, ff = x_ref.shape[1], hid.shape[1]
    parts_up, parts_down = sem_up.shape[0], sem_down.shape[0]
    ups = [slice(c * ff // parts_up, (c + 1) * ff // parts_up) for c in range(parts_up)]
    downs = [slice(c * width // parts_down, (c + 1) * width // parts_down) for c in range(parts_down)]
    copies_up = [
        pltpu.make_async_copy(up_hbm.at[part], up_ref.at[part], sem_up.at[c])
        for c, part in enumerate(ups)
    ]
    copies_down = [
        pltpu.make_async_copy(down_hbm.at[part], down_ref.at[part], sem_down.at[c])
        for c, part in enumerate(downs)
    ]
    for copy in copies_up + copies_down:
        copy.start()
    x = x_ref[...]
    for copy, part in zip(copies_up, ups):
        copy.wait()
        gate = lax.dot_general(x, up_ref[part, :width], NT, preferred_element_type=F32)
        upper = lax.dot_general(x, up_ref[part, width:], NT, preferred_element_type=F32)
        hid[:, part] = (gate / (1.0 + jnp.exp(-gate)) * upper).astype(BF16)
    hidden = hid[...]
    for copy, part in zip(copies_down, downs):
        copy.wait()
        out_ref[:, part] = lax.dot_general(
            hidden, down_ref[part], NT, preferred_element_type=F32
        ).astype(BF16)


def last_kernel(expert_ref, probs_ref, x_ref, out_ref, *, ring, cap):
    expert = expert_ref[...]
    count = expert.shape[0]
    member = lax.broadcasted_iota(jnp.int32, (count, ring), 1) == expert
    before = lax.broadcasted_iota(jnp.int32, (count, count), 1) < lax.broadcasted_iota(
        jnp.int32, (count, count), 0
    )
    earlier = lax.dot_general(
        before.astype(F32), member.astype(F32), NN, preferred_element_type=F32
    )
    slot = jnp.sum(jnp.where(member, earlier, 0.0), axis=1, keepdims=True).astype(jnp.int32)
    place = expert * cap + slot
    pick = lax.broadcasted_iota(jnp.int32, (count, ring * cap), 1) == place
    probs = probs_ref[...]
    share = probs[:, :1] / jnp.sum(probs, axis=1, keepdims=True)
    got = lax.dot_general(
        pick.astype(F32).astype(BF16), x_ref[...], NN, preferred_element_type=F32
    )
    out_ref[...] = (share * got).astype(BF16)


def exchange(x, ring):
    blocks = x.reshape(ring, x.shape[0] // ring, x.shape[1])
    return lax.all_to_all(blocks, "expert", split_axis=0, concat_axis=0, tiled=True).reshape(x.shape)


def local(tokens, norm_gain, route_probs, window_expert, w_gate_up, w_down):
    tok_count, width = tokens.shape
    ring = lax.axis_size("expert")
    cap = 3 * tok_count // ring
    rows = ring * cap
    ff = w_down.shape[2]
    sent = pl.pallas_call(
        functools.partial(send_kernel, ring=ring, cap=cap),
        out_shape=jax.ShapeDtypeStruct((rows, width), BF16),
        in_specs=[VMEM] * 3,
        out_specs=VMEM,
        compiler_params=pltpu.CompilerParams(vmem_limit_bytes=20 << 20),
        cost_estimate=pl.CostEstimate(
            flops=6 * tok_count * tok_count * width,
            bytes_accessed=8 * tokens.size,
            transcendentals=0,
        ),
        name="send",
    )(tokens, norm_gain[None, :], window_expert[None, :])
    x = exchange(sent, ring)
    up, down = arrange(gather(w_gate_up, X_STEPS + Y_STEPS), gather(w_down, Y_STEPS + X_STEPS))
    made = pl.pallas_call(
        expert_kernel,
        out_shape=jax.ShapeDtypeStruct((rows, width), BF16),
        in_specs=[VMEM, HBM, HBM],
        out_specs=VMEM,
        scratch_shapes=[
            pltpu.VMEM((ff, 2 * width), BF16),
            pltpu.VMEM((width, ff), BF16),
            pltpu.VMEM((rows, ff), BF16),
            pltpu.SemaphoreType.DMA((3,)),
            pltpu.SemaphoreType.DMA((4,)),
        ],
        compiler_params=pltpu.CompilerParams(vmem_limit_bytes=55 << 20),
        cost_estimate=pl.CostEstimate(
            flops=6 * rows * width * ff,
            bytes_accessed=6 * width * ff + 4 * x.size,
            transcendentals=rows * ff,
        ),
        name="expert",
    )(x, up.reshape(ff, 2 * width), down.reshape(width, ff))
    return pl.pallas_call(
        functools.partial(last_kernel, ring=ring, cap=cap),
        out_shape=jax.ShapeDtypeStruct((tok_count, width), BF16),
        in_specs=[VMEM] * 3,
        out_specs=VMEM,
        cost_estimate=pl.CostEstimate(
            flops=6 * tok_count * tok_count * width, bytes_accessed=8 * tokens.size, transcendentals=0
        ),
        compiler_params=pltpu.CompilerParams(vmem_limit_bytes=16 << 20),
        name="last",
    )(window_expert[:, None], route_probs, exchange(made, ring))


def solution(mesh):
    placed = (
        P(("dp", "expert"), None),
        P(),
        P(("dp", "expert"), None),
        P(("dp", "expert")),
        P("expert", "dp", None),
        P("expert", "dp", None),
    )
    return jax.shard_map(
        local, mesh=mesh, in_specs=placed, out_specs=P(("dp", "expert"), None), check_vma=False
    )
```

time: 245 us -> 517 us (2.11)
  Pallas kernels: 0 us -> 301 us
  starting transfers between devices: 27.7 us -> 60.6 us
  waiting for transfers between devices: 181 us -> 150 us
  between operations: 13.5 us -> 0.36 us
  matrix products: 10.5 us -> 0 us
  other arithmetic: 7.39 us -> 0.18 us
    pallas_call x0 -> x4, Pallas kernels: none -> 301 us  [the longest x1 288 us: arrange(): pl.pallas_call(arrange_kernel, out_shape=[jax.ShapeDtypeStruct(shape, BF1...]
    ppermute x0 -> x12, waiting for transfers between devices: none -> 75.3 us  [trade(): lax.ppermute(x, 'dp', [(i, i ^ mask) for i in range(lax.axis_size('dp'))])]
    all_to_all x2, waiting for transfers between devices: 148 us -> 74.3 us  [exchange(): lax.all_to_all(blocks, 'expert', split_axis=0, concat_axis=0, tiled=True)]
    ppermute x0 -> x12, starting transfers between devices: none -> 34.5 us  [trade(): lax.ppermute(x, 'dp', [(i, i ^ mask) for i in range(lax.axis_size('dp'))])]
    all_gather x2 -> x0, waiting for transfers between devices: 31.4 us -> none  [the longest x1 31.4 us: local(): lax.all_gather(w_down[0], 'dp', axis=0, tiled=True)]
    dot_general x2 -> x0, matrix products: 10.5 us -> none  [the longest x1 7.14 us: local(): lax.dot_general(hidden, lax.all_gather(w_down[0], 'dp', axis=0, tiled=Tru...]
  transfers between devices with their start and end apart: 4 -> 14, of which waited for: 3 -> 8; matrix products, arithmetic and copies ran while one was open for 5% -> 0% of each run, Pallas kernels for 0% -> 56%
where the time goes in v2:
time: 517 us; the launch traced here: 516 us
  Pallas kernels  301 us (58%)
  waiting for transfers between devices  150 us (29%)
  starting transfers between devices  60.6 us (12%)
    pallas_call x1, Pallas kernels, arrange(): pl.pallas_call(arrange_kernel, out_shape=[jax.ShapeDtypeStruct(shape, BF1...  288 us
    ppermute x12, waiting for transfers between devices, trade(): lax.ppermute(x, 'dp', [(i, i ^ mask) for i in range(lax.axis_size('dp'))])  75.3 us
    all_to_all x2, waiting for transfers between devices, exchange(): lax.all_to_all(blocks, 'expert', split_axis=0, concat_axis=0, tiled=True)  74.3 us
    ppermute x12, starting transfers between devices, trade(): lax.ppermute(x, 'dp', [(i, i ^ mask) for i in range(lax.axis_size('dp'))])  34.5 us
    all_to_all x2, starting transfers between devices, exchange(): lax.all_to_all(blocks, 'expert', split_axis=0, concat_axis=0, tiled=True)  26.1 us
  transfers between devices with their start and end apart: 14, of which 8 were waited for; matrix products, arithmetic and copies ran while one was open for 0% of the time, Pallas kernels for 56%

profile of v2, /device:TPU:24, one launch (start us, length us, event | category | flops | bytes accessed | tf_op | source)
XLA Modules:
  0.0 516.3 jit_solution(237804370250728623)
XLA Ops:
  0.0 3.4 collective-permute-start
  3.4 0.0 copy-start
  3.4 1.0 copy-done
  4.4 0.7 copy-done.1
  5.1 0.7 copy-done.2
  5.8 1.9 send.1
  7.7 15.4 %all-to-all-start = ((bf16[16,24,2048]{2,1,0:T(8,128)(2,1)}), bf16[16,24,2048]{2,1,0:T(8,128)(2,1)}, u32[]{:S(2)}, u32[]{:S(2)}) async-start(bf16[16,24,2048]{2,1,0:T(8,128)(2,1)} %bitcast.3), calls=%async_computation | async-start | bytes 3145728 | tf_op jit(solution)/shard_map/all_to_all | solution.py:151
  23.1 0.0 collective-permute-done
  23.2 4.0 collective-permute-start.1
  27.2 9.4 %collective-permute-done.1 = bf16[2,24,4096]{2,1,0:T(8,128)(2,1)S(1)} collective-permute-done((bf16[2,24,4096]{2,1,0:T(8,128)(2,1)S(1)}, bf16[2,24,4096]{2,1,0:T(8,128)(2,1)S(1)}, u32[]{:S(2)}, u32[]{:S(2)}) %collective-permute-start.1) | collective-permute-done | bytes 393248 | tf_op jit(solution)/shard_map/ppermute | solution.py:19
  36.6 0.1 pad_maximum_fusion
  36.7 0.0 copy-start.9
  36.7 2.8 collective-permute-start.2
  39.5 17.1 %collective-permute-done.2 = bf16[4,24,4096]{2,1,0:T(8,128)(2,1)S(1)} collective-permute-done((bf16[4,24,4096]{2,1,0:T(8,128)(2,1)S(1)}, bf16[4,24,4096]{2,1,0:T(8,128)(2,1)S(1)}, u32[]{:S(2)}, u32[]{:S(2)}) %collective-permute-start.2) | collective-permute-done | bytes 786464 | tf_op jit(solution)/shard_map/ppermute | solution.py:19
  56.6 0.1 constant_dynamic-update-slice_fusion.refs_0_
  56.7 2.1 collective-permute-start.3
  58.8 2.9 collective-permute-start.6
  61.7 3.6 collective-permute-done.6
  65.3 4.9 collective-permute-start.7
  70.3 27.6 %collective-permute-done.7 = bf16[2,64,768]{2,1,0:T(8,128)(2,1)S(1)} collective-permute-done((bf16[2,64,768]{2,1,0:T(8,128)(2,1)S(1)}, bf16[2,64,768]{2,1,0:T(8,128)(2,1)S(1)}, u32[]{:S(2)}, u32[]{:S(2)}) %collective-permute-start.7) | collective-permute-done | bytes 196640 | tf_op jit(solution)/shard_map/ppermute | solution.py:19
  98.0 2.3 collective-permute-start.8
  100.3 7.4 %collective-permute-done.8 = bf16[4,64,768]{2,1,0:T(8,128)(2,1)S(1)} collective-permute-done((bf16[4,64,768]{2,1,0:T(8,128)(2,1)S(1)}, bf16[4,64,768]{2,1,0:T(8,128)(2,1)S(1)}, u32[]{:S(2)}, u32[]{:S(2)}) %collective-permute-start.8) | collective-permute-done | bytes 393248 | tf_op jit(solution)/shard_map/ppermute | solution.py:19
  107.8 4.0 collective-permute-start.9
  111.7 1.9 collective-permute-start.4
  113.7 0.0 collective-permute-done.3.refs_1_
  113.7 2.4 collective-permute-start.5
  116.1 1.9 collective-permute-start.10
  118.0 7.9 %collective-permute-done.9.refs_5_ = bf16[8,64,768]{2,1,0:T(8,128)(2,1)S(1)} collective-permute-done((bf16[8,64,768]{2,1,0:T(8,128)(2,1)S(1)}, bf16[8,64,768]{2,1,0:T(8,128)(2,1)S(1)}, u32[]{:S(2)}, u32[]{:S(2)}) %collective-permute-start.9) | collective-permute-done | bytes 786464 | tf_op jit(solution)/shard_map/ppermute | solution.py:19
  125.9 1.9 collective-permute-start.11
  127.8 0.0 collective-permute-done.10.refs_6_
  127.9 2.2 collective-permute-done.11.refs_7_
  130.1 0.0 collective-permute-done.4.refs_2_
  130.1 0.0 copy-done.8
  130.1 0.9 copy-done.12
  131.0 1.2 copy-done.7
  132.2 0.0 collective-permute-done.5.refs_3_
  132.2 0.0 copy-done.6
  132.2 287.6 %arrange.1 = (bf16[32,24,4096]{2,1,0:T(8,128)(2,1)}, bf16[32,64,768]{2,1,0:T(8,128)(2,1)}) custom-call(bf16[8,24,4096]{2,1,0:T(8,128)(2,1)} %copy-done.4, bf16[8,24,4096]{2,1,0:T(8,128)(2,1)} %copy-done.6, bf16[8,24,4096]{2,1,0:T(8,128)(2,1)} %copy-done.7, bf16[8,24,4096]{2,1,0:T(8,128)(2,1)} %collective-permute-done.5.refs_3_, ...), custom_call_target="tpu_custom_call" | custom-call | bytes 19922944 | tf_op jit(solution)/shard_map/arrange/pallas_call | solution.py:88
  419.7 0.0 all-to-all-done
  419.8 9.6 %expert.1 = bf16[384,2048]{1,0:T(8,128)(2,1)} custom-call(bf16[384,2048]{1,0:T(8,128)(2,1)} %bitcast.4.x_ref, bf16[768,4096]{1,0:T(8,128)(2,1)} %bitcast.14, bf16[2048,768]{1,0:T(8,128)(2,1)} %bitcast.15), custom_call_target="tpu_custom_call" | custom-call | flops 3623878656 | bytes 12582912 | tf_op jit(solution)/shard_map/expert/pallas_call | solution.py:175
  429.4 0.0 copy-start.3
  429.4 0.0 copy-start.13
  429.4 10.8 %all-to-all-start.1 = ((bf16[16,24,2048]{2,1,0:T(8,128)(2,1)}), bf16[16,24,2048]{2,1,0:T(8,128)(2,1)S(1)}, u32[]{:S(2)}, u32[]{:S(2)}) async-start(bf16[16,24,2048]{2,1,0:T(8,128)(2,1)} %bitcast.13), calls=%async_computation.1 | async-start | bytes 3145728 | tf_op jit(solution)/shard_map/all_to_all | solution.py:151
  440.2 0.1 copy.7.expert_ref
  440.3 0.0 copy-done.13
  440.3 0.1 copy.8.probs_ref
  440.4 74.3 %all-to-all-done.1 = bf16[16,24,2048]{2,1,0:T(8,128)(2,1)S(1)} async-done(((bf16[16,24,2048]{2,1,0:T(8,128)(2,1)}), bf16[16,24,2048]{2,1,0:T(8,128)(2,1)S(1)}, u32[]{:S(2)}, u32[]{:S(2)}) %all-to-all-start.1) | async-done | bytes 1572896 | tf_op jit(solution)/shard_map/all_to_all | solution.py:151
  514.7 1.6 last.1
  (26 shorter events, 0.2 us)
Async XLA Ops:
  0.0 23.1 %collective-permute-start = (bf16[1,24,4096]{2,1,0:T(8,128)(2,1)}, bf16[1,24,4096]{2,1,0:T(8,128)(2,1)S(1)}, u32[]{:S(2)}, u32[]{:S(2)}) collective-permute-start(bf16[1,24,4096]{2,1,0:T(8,128)(2,1)} %param.10), channel_id=1, source_target_pairs={{0,128},{16,144},{32,160},{48,176},{64,192},{80,208},{96,224},{112... | collective-permute-start | bytes 589832 | tf_op jit(solution)/shard_map/ppermute | solution.py:19
  3.4 1.0 copy-start
  4.4 0.7 copy-start.1
  5.1 0.7 copy-start.2
  7.7 15.4 %copy-start.5 = (bf16[1,24,4096]{2,1,0:T(8,128)(2,1)S(1)}, bf16[1,24,4096]{2,1,0:T(8,128)(2,1)}, u32[]{:S(2)}) copy-start(bf16[1,24,4096]{2,1,0:T(8,128)(2,1)} %param.10) | copy-start | bytes 589828
  7.7 412.0 %all-to-all-start = ((bf16[16,24,2048]{2,1,0:T(8,128)(2,1)}), bf16[16,24,2048]{2,1,0:T(8,128)(2,1)}, u32[]{:S(2)}, u32[]{:S(2)}) async-start(bf16[16,24,2048]{2,1,0:T(8,128)(2,1)} %bitcast.3), calls=%async_computation | async-start | bytes 3145728 | tf_op jit(solution)/shard_map/all_to_all | solution.py:151
  23.2 13.4 %collective-permute-start.1 = (bf16[2,24,4096]{2,1,0:T(8,128)(2,1)S(1)}, bf16[2,24,4096]{2,1,0:T(8,128)(2,1)S(1)}, u32[]{:S(2)}, u32[]{:S(2)}) collective-permute-start(bf16[2,24,4096]{2,1,0:T(8,128)(2,1)S(1)} %pad_maximum_fusion.1), channel_id=1, source_target_pairs={{0,384},{16,400},{32,416},{48,432},{64,448},{80,464},{96,480},{112... | collective-permute-start | bytes 1179656 | tf_op jit(solution)/shard_map/ppermute | solution.py:19
  36.7 22.1 %copy-start.9 = (bf16[1,64,768]{2,1,0:T(8,128)(2,1)S(1)}, bf16[1,64,768]{2,1,0:T(8,128)(2,1)}, u32[]{:S(2)}) copy-start(bf16[1,64,768]{2,1,0:T(8,128)(2,1)} %param.11) | copy-start | bytes 294916
  36.7 19.9 %collective-permute-start.2 = (bf16[4,24,4096]{2,1,0:T(8,128)(2,1)S(1)}, bf16[4,24,4096]{2,1,0:T(8,128)(2,1)S(1)}, u32[]{:S(2)}, u32[]{:S(2)}) collective-permute-start(bf16[4,24,4096]{2,1,0:T(8,128)(2,1)S(1)} %pad_maximum_fusion), channel_id=1, source_target_pairs={{0,32},{16,48},{32,0},{48,16},{64,96},{80,112},{96,64},{112,80},{1... | collective-permute-start | bytes 2359304 | tf_op jit(solution)/shard_map/ppermute | solution.py:19
  56.7 75.5 %copy-start.4 = (bf16[8,24,4096]{2,1,0:T(8,128)(2,1)}, bf16[8,24,4096]{2,1,0:T(8,128)(2,1)S(1)}, u32[]{:S(2)}) copy-start(bf16[8,24,4096]{2,1,0:T(8,128)(2,1)S(1)} %constant_dynamic-update-slice_fusion.refs_0_) | copy-start | bytes 4718596
  56.7 57.0 %collective-permute-start.3 = (bf16[8,24,4096]{2,1,0:T(8,128)(2,1)S(1)}, bf16[8,24,4096]{2,1,0:T(8,128)(2,1)S(1)}, u32[]{:S(2)}, u32[]{:S(2)}) collective-permute-start(bf16[8,24,4096]{2,1,0:T(8,128)(2,1)S(1)} %constant_dynamic-update-slice_fusion.refs_0_), channel_id=1, source_target_pairs={{0,96},{16,112},{32,64},{48,80},{64,32},{80,48},{96,0},{112,16},{1... | collective-permute-start | bytes 4718600 | tf_op jit(solution)/shard_map/ppermute | solution.py:19
  58.8 6.5 %collective-permute-start.6 = (bf16[1,64,768]{2,1,0:T(8,128)(2,1)S(1)}, bf16[1,64,768]{2,1,0:T(8,128)(2,1)S(1)}, u32[]{:S(2)}, u32[]{:S(2)}) collective-permute-start(bf16[1,64,768]{2,1,0:T(8,128)(2,1)S(1)} %copy-done.9), channel_id=1, source_target_pairs={{0,32},{16,48},{32,0},{48,16},{64,96},{80,112},{96,64},{112,80},{1... | collective-permute-start | bytes 294920 | tf_op jit(solution)/shard_map/ppermute | solution.py:19
  65.3 32.6 %collective-permute-start.7 = (bf16[2,64,768]{2,1,0:T(8,128)(2,1)S(1)}, bf16[2,64,768]{2,1,0:T(8,128)(2,1)S(1)}, u32[]{:S(2)}, u32[]{:S(2)}) collective-permute-start(bf16[2,64,768]{2,1,0:T(8,128)(2,1)S(1)} %pad_maximum_fusion.3), channel_id=1, source_target_pairs={{0,96},{16,112},{32,64},{48,80},{64,32},{80,48},{96,0},{112,16},{1... | collective-permute-start | bytes 589832 | tf_op jit(solution)/shard_map/ppermute | solution.py:19
  98.0 9.7 %collective-permute-start.8 = (bf16[4,64,768]{2,1,0:T(8,128)(2,1)S(1)}, bf16[4,64,768]{2,1,0:T(8,128)(2,1)S(1)}, u32[]{:S(2)}, u32[]{:S(2)}) collective-permute-start(bf16[4,64,768]{2,1,0:T(8,128)(2,1)S(1)} %pad_maximum_fusion.2), channel_id=1, source_target_pairs={{0,128},{16,144},{32,160},{48,176},{64,192},{80,208},{96,224},{112... | collective-permute-start | bytes 1179656 | tf_op jit(solution)/shard_map/ppermute | solution.py:19
  107.7 22.3 %copy-start.8 = (bf16[8,64,768]{2,1,0:T(8,128)(2,1)}, bf16[8,64,768]{2,1,0:T(8,128)(2,1)S(1)}, u32[]{:S(2)}) copy-start(bf16[8,64,768]{2,1,0:T(8,128)(2,1)S(1)} %constant_dynamic-update-slice_fusion.4.refs_4_) | copy-start | bytes 2359300
  107.8 18.2 %collective-permute-start.9 = (bf16[8,64,768]{2,1,0:T(8,128)(2,1)S(1)}, bf16[8,64,768]{2,1,0:T(8,128)(2,1)S(1)}, u32[]{:S(2)}, u32[]{:S(2)}) collective-permute-start(bf16[8,64,768]{2,1,0:T(8,128)(2,1)S(1)} %constant_dynamic-update-slice_fusion.4.refs_4_), channel_id=1, source_target_pairs={{0,384},{16,400},{32,416},{48,432},{64,448},{80,464},{96,480},{112... | collective-permute-start | bytes 2359304 | tf_op jit(solution)/shard_map/ppermute | solution.py:19
  111.7 18.4 %collective-permute-start.4 = (bf16[8,24,4096]{2,1,0:T(8,128)(2,1)S(1)}, bf16[8,24,4096]{2,1,0:T(8,128)(2,1)S(1)}, u32[]{:S(2)}, u32[]{:S(2)}) collective-permute-start(bf16[8,24,4096]{2,1,0:T(8,128)(2,1)S(1)} %constant_dynamic-update-slice_fusion.refs_0_), channel_id=1, source_target_pairs={{0,16},{16,0},{32,48},{48,32},{64,80},{80,64},{96,112},{112,96},{1... | collective-permute-start | bytes 4718600 | tf_op jit(solution)/shard_map/ppermute | solution.py:19
  113.7 18.5 %copy-start.6 = (bf16[8,24,4096]{2,1,0:T(8,128)(2,1)}, bf16[8,24,4096]{2,1,0:T(8,128)(2,1)S(1)}, u32[]{:S(2)}) copy-start(bf16[8,24,4096]{2,1,0:T(8,128)(2,1)S(1)} %collective-permute-done.3.refs_1_) | copy-start | bytes 4718596
  113.7 18.5 %collective-permute-start.5 = (bf16[8,24,4096]{2,1,0:T(8,128)(2,1)S(1)}, bf16[8,24,4096]{2,1,0:T(8,128)(2,1)}, u32[]{:S(2)}, u32[]{:S(2)}) collective-permute-start(bf16[8,24,4096]{2,1,0:T(8,128)(2,1)S(1)} %collective-permute-done.3.refs_1_), channel_id=1, source_target_pairs={{0,16},{16,0},{32,48},{48,32},{64,80},{80,64},{96,112},{112,96},{1... | collective-permute-start | bytes 4718600 | tf_op jit(solution)/shard_map/ppermute | solution.py:19
  116.1 11.7 %collective-permute-start.10 = (bf16[8,64,768]{2,1,0:T(8,128)(2,1)S(1)}, bf16[8,64,768]{2,1,0:T(8,128)(2,1)S(1)}, u32[]{:S(2)}, u32[]{:S(2)}) collective-permute-start(bf16[8,64,768]{2,1,0:T(8,128)(2,1)S(1)} %constant_dynamic-update-slice_fusion.4.refs_4_), channel_id=1, source_target_pairs={{0,16},{16,0},{32,48},{48,32},{64,80},{80,64},{96,112},{112,96},{1... | collective-permute-start | bytes 2359304 | tf_op jit(solution)/shard_map/ppermute | solution.py:19
  125.9 4.2 copy-start.10
  125.9 4.2 collective-permute-start.11
  127.8 2.3 copy-start.11
  130.1 0.9 copy-start.12
  131.0 1.2 copy-start.7
  429.4 10.8 %copy-start.3 = (s32[128]{0:T(128)S(1)}, s32[128]{0:T(128)}, u32[]{:S(2)}) copy-start(s32[128]{0:T(128)} %param.9) | copy-start | bytes 1540
  429.4 10.9 %copy-start.13 = (f32[128,8]{0,1:T(8,128)S(1)}, f32[128,8]{0,1:T(8,128)}, u32[]{:S(2)}) copy-start(f32[128,8]{0,1:T(8,128)} %param.8) | copy-start | bytes 12292
  429.4 85.3 %all-to-all-start.1 = ((bf16[16,24,2048]{2,1,0:T(8,128)(2,1)}), bf16[16,24,2048]{2,1,0:T(8,128)(2,1)S(1)}, u32[]{:S(2)}, u32[]{:S(2)}) async-start(bf16[16,24,2048]{2,1,0:T(8,128)(2,1)} %bitcast.13), calls=%async_computation.1 | async-start | bytes 3145728 | tf_op jit(solution)/shard_map/all_to_all | solution.py:151

commit v3 on v2

--- a/solution.py
+++ b/solution.py
@@ -22,11 +22,15 @@
 X_STEPS, Y_STEPS, CORE = (8, 24), (2, 6), 1
 
 
-def gather(x, steps):
-    for mask in steps[:-1]:
-        x = jnp.concatenate([x, trade(x, mask)], axis=0)
-    y = trade(x, steps[-1])
-    return x, y, trade(x, CORE), trade(y, CORE)
+def gather(a, b):
+    a_steps, b_steps = X_STEPS + Y_STEPS, Y_STEPS + X_STEPS
+    for a_mask, b_mask in zip(a_steps[:-1], b_steps[:-1]):
+        a_in, b_in = lax.optimization_barrier((trade(a, a_mask), trade(b, b_mask)))
+        a, b = jnp.concatenate([a, a_in], axis=0), jnp.concatenate([b, b_in], axis=0)
+    a_in, b_in, a_near, b_near = lax.optimization_barrier(
+        (trade(a, a_steps[-1]), trade(b, b_steps[-1]), trade(a, CORE), trade(b, CORE))
+    )
+    return (a, a_in, a_near, trade(a_in, CORE)), (b, b_in, b_near, trade(b_in, CORE))
 
 
 def gray(k):
@@ -89,7 +93,8 @@
         arrange_kernel,
         out_shape=[jax.ShapeDtypeStruct(shape, BF16) for shape in shapes],
         in_specs=[ANY] * 8,
-        out_specs=[HBM] * 2,
+        out_specs=[VMEM] * 2,
+        compiler_params=pltpu.CompilerParams(vmem_limit_bytes=20 << 20),
         scratch_shapes=[pltpu.SemaphoreType.DMA((shapes[0][0],))] * 2,
         cost_estimate=pl.CostEstimate(flops=0, bytes_accessed=38 << 19, transcendentals=0),
         name="arrange",
@@ -171,7 +176,7 @@
         name="send",
     )(tokens, norm_gain[None, :], window_expert[None, :])
     x = exchange(sent, ring)
-    up, down = arrange(gather(w_gate_up, X_STEPS + Y_STEPS), gather(w_down, Y_STEPS + X_STEPS))
+    up, down = arrange(*gather(w_gate_up, w_down))
     made = pl.pallas_call(
         expert_kernel,
         out_shape=jax.ShapeDtypeStruct((rows, width), BF16),

time: 517 us -> 218 us (0.42)
  Pallas kernels: 301 us -> 25.9 us
  waiting for transfers between devices: 150 us -> 122 us
    pallas_call x1, Pallas kernels: 288 us -> 12.9 us  [arrange(): pl.pallas_call(arrange_kernel, out_shape=[jax.ShapeDtypeStruct(shape, BF1...]
    ppermute x12, waiting for transfers between devices: 75.3 us -> 47.8 us  [trade(): lax.ppermute(x, 'dp', [(i, i ^ mask) for i in range(lax.axis_size('dp'))])]
  transfers between devices with their start and end apart: 14 -> 14, of which waited for: 8 -> 8; matrix products, arithmetic and copies ran while one was open for 0% -> 0% of each run, Pallas kernels for 56% -> 6%
where the time goes in v3:
time: 218 us; the launch traced here: 217 us
  waiting for transfers between devices  122 us (56%)
  starting transfers between devices  60 us (28%)
  Pallas kernels  25.9 us (12%)
  local copies, waits for them, and re-layouts  8.32 us (4%)
    all_to_all x2, waiting for transfers between devices, exchange(): lax.all_to_all(blocks, 'expert', split_axis=0, concat_axis=0, tiled=True)  74.4 us
    ppermute x12, waiting for transfers between devices, trade(): lax.ppermute(x, 'dp', [(i, i ^ mask) for i in range(lax.axis_size('dp'))])  47.8 us
    ppermute x12, starting transfers between devices, trade(): lax.ppermute(x, 'dp', [(i, i ^ mask) for i in range(lax.axis_size('dp'))])  33.4 us
    all_to_all x2, starting transfers between devices, exchange(): lax.all_to_all(blocks, 'expert', split_axis=0, concat_axis=0, tiled=True)  26.5 us
    pallas_call x1, Pallas kernels, arrange(): pl.pallas_call(arrange_kernel, out_shape=[jax.ShapeDtypeStruct(shape, BF1...  12.9 us
    pallas_call x1, Pallas kernels, local(): pl.pallas_call(expert_kernel, out_shape=jax.ShapeDtypeStruct((rows, width...  9.59 us
    unnamed x27, local copies, waits for them, and re-layouts  8.13 us
  transfers between devices with their start and end apart: 14, of which 8 were waited for; matrix products, arithmetic and copies ran while one was open for 0% of the time, Pallas kernels for 6%

profile of v3, /device:TPU:24, one launch (start us, length us, event | category | flops | bytes accessed | tf_op | source)
XLA Modules:
  0.0 216.8 jit_solution(1916397514487493069)
XLA Ops:
  0.0 3.4 %collective-permute-start = (bf16[1,24,4096]{2,1,0:T(8,128)(2,1)}, bf16[1,24,4096]{2,1,0:T(8,128)(2,1)S(1)}, u32[]{:S(2)}, u32[]{:S(2)}) collective-permute-start(bf16[1,24,4096]{2,1,0:T(8,128)(2,1)} %param.10), channel_id=1, source_target_pairs={{0,128},{16,144},{32,160},{48,176},{64,192},{80,208},{96,224},{112... | collective-permute-start | bytes 589832 | tf_op jit(solution)/shard_map/ppermute | solution.py:19
  3.4 2.7 %collective-permute-start.1 = (bf16[1,64,768]{2,1,0:T(8,128)(2,1)}, bf16[1,64,768]{2,1,0:T(8,128)(2,1)S(1)}, u32[]{:S(2)}, u32[]{:S(2)}) collective-permute-start(bf16[1,64,768]{2,1,0:T(8,128)(2,1)} %param.11), channel_id=1, source_target_pairs={{0,32},{16,48},{32,0},{48,16},{64,96},{80,112},{96,64},{112,80},{1... | collective-permute-start | bytes 294920 | tf_op jit(solution)/shard_map/ppermute | solution.py:19
  6.1 0.0 copy-start
  6.1 1.0 copy-done
  7.1 0.7 copy-done.1
  7.8 0.7 copy-done.2
  8.5 1.9 send.1
  10.4 15.3 %all-to-all-start = ((bf16[16,24,2048]{2,1,0:T(8,128)(2,1)}), bf16[16,24,2048]{2,1,0:T(8,128)(2,1)S(1)}, u32[]{:S(2)}, u32[]{:S(2)}) async-start(bf16[16,24,2048]{2,1,0:T(8,128)(2,1)} %bitcast.3), calls=%async_computation | async-start | bytes 3145728 | tf_op jit(solution)/shard_map/all_to_all | solution.py:156
  25.7 0.0 collective-permute-done.1
  25.7 0.0 collective-permute-done
  25.7 0.0 copy-done.6
  25.8 4.0 %collective-permute-start.2 = (bf16[2,24,4096]{2,1,0:T(8,128)(2,1)S(1)}, bf16[2,24,4096]{2,1,0:T(8,128)(2,1)S(1)}, u32[]{:S(2)}, u32[]{:S(2)}) collective-permute-start(bf16[2,24,4096]{2,1,0:T(8,128)(2,1)S(1)} %pad_maximum_fusion.1), channel_id=1, source_target_pairs={{0,384},{16,400},{32,416},{48,432},{64,448},{80,464},{96,480},{112... | collective-permute-start | bytes 1179656 | tf_op jit(solution)/shard_map/ppermute | solution.py:19
  29.8 0.0 copy-done.8
  29.8 3.0 %collective-permute-start.3 = (bf16[2,64,768]{2,1,0:T(8,128)(2,1)S(1)}, bf16[2,64,768]{2,1,0:T(8,128)(2,1)S(1)}, u32[]{:S(2)}, u32[]{:S(2)}) collective-permute-start(bf16[2,64,768]{2,1,0:T(8,128)(2,1)S(1)} %pad_maximum_fusion.3), channel_id=1, source_target_pairs={{0,96},{16,112},{32,64},{48,80},{64,32},{80,48},{96,0},{112,16},{1... | collective-permute-start | bytes 589832 | tf_op jit(solution)/shard_map/ppermute | solution.py:19
  32.8 5.8 %collective-permute-done.3 = bf16[2,64,768]{2,1,0:T(8,128)(2,1)S(1)} collective-permute-done((bf16[2,64,768]{2,1,0:T(8,128)(2,1)S(1)}, bf16[2,64,768]{2,1,0:T(8,128)(2,1)S(1)}, u32[]{:S(2)}, u32[]{:S(2)}) %collective-permute-start.3) | collective-permute-done | bytes 196640 | tf_op jit(solution)/shard_map/ppermute | solution.py:19
  38.6 0.3 collective-permute-done.2
  38.9 0.1 pad_maximum_fusion
  39.0 3.2 %collective-permute-start.4 = (bf16[4,24,4096]{2,1,0:T(8,128)(2,1)S(1)}, bf16[4,24,4096]{2,1,0:T(8,128)(2,1)S(1)}, u32[]{:S(2)}, u32[]{:S(2)}) collective-permute-start(bf16[4,24,4096]{2,1,0:T(8,128)(2,1)S(1)} %pad_maximum_fusion), channel_id=1, source_target_pairs={{0,32},{16,48},{32,0},{48,16},{64,96},{80,112},{96,64},{112,80},{1... | collective-permute-start | bytes 2359304 | tf_op jit(solution)/shard_map/ppermute | solution.py:19
  42.3 1.9 collective-permute-start.5
  44.2 8.7 %collective-permute-done.5 = bf16[4,64,768]{2,1,0:T(8,128)(2,1)S(1)} collective-permute-done((bf16[4,64,768]{2,1,0:T(8,128)(2,1)S(1)}, bf16[4,64,768]{2,1,0:T(8,128)(2,1)S(1)}, u32[]{:S(2)}, u32[]{:S(2)}) %collective-permute-start.5) | collective-permute-done | bytes 393248 | tf_op jit(solution)/shard_map/ppermute | solution.py:19
  53.0 5.4 %collective-permute-done.4 = bf16[4,24,4096]{2,1,0:T(8,128)(2,1)S(1)} collective-permute-done((bf16[4,24,4096]{2,1,0:T(8,128)(2,1)S(1)}, bf16[4,24,4096]{2,1,0:T(8,128)(2,1)S(1)}, u32[]{:S(2)}, u32[]{:S(2)}) %collective-permute-start.4) | collective-permute-done | bytes 786464 | tf_op jit(solution)/shard_map/ppermute | solution.py:19
  58.4 0.1 constant_dynamic-update-slice_fusion.refs_0_
  58.5 3.0 %collective-permute-start.6 = (bf16[8,24,4096]{2,1,0:T(8,128)(2,1)S(1)}, bf16[8,24,4096]{2,1,0:T(8,128)(2,1)S(1)}, u32[]{:S(2)}, u32[]{:S(2)}) collective-permute-start(bf16[8,24,4096]{2,1,0:T(8,128)(2,1)S(1)} %constant_dynamic-update-slice_fusion.refs_0_), channel_id=1, source_target_pairs={{0,96},{16,112},{32,64},{48,80},{64,32},{80,48},{96,0},{112,16},{1... | collective-permute-start | bytes 4718600 | tf_op jit(solution)/shard_map/ppermute | solution.py:19
  61.4 1.9 collective-permute-start.8
  63.4 4.0 %collective-permute-start.7 = (bf16[8,64,768]{2,1,0:T(8,128)(2,1)S(1)}, bf16[8,64,768]{2,1,0:T(8,128)(2,1)S(1)}, u32[]{:S(2)}, u32[]{:S(2)}) collective-permute-start(bf16[8,64,768]{2,1,0:T(8,128)(2,1)S(1)} %constant_dynamic-update-slice_fusion.4.refs_4_), channel_id=1, source_target_pairs={{0,384},{16,400},{32,416},{48,432},{64,448},{80,464},{96,480},{112... | collective-permute-start | bytes 2359304 | tf_op jit(solution)/shard_map/ppermute | solution.py:19
  67.4 2.1 collective-permute-start.9
  69.6 16.9 %collective-permute-done.7.refs_5_ = bf16[8,64,768]{2,1,0:T(8,128)(2,1)S(1)} collective-permute-done((bf16[8,64,768]{2,1,0:T(8,128)(2,1)S(1)}, bf16[8,64,768]{2,1,0:T(8,128)(2,1)S(1)}, u32[]{:S(2)}, u32[]{:S(2)}) %collective-permute-start.7) | collective-permute-done | bytes 786464 | tf_op jit(solution)/shard_map/ppermute | solution.py:19
  86.5 0.0 collective-permute-done.9.refs_6_
  86.5 8.5 %collective-permute-done.6.refs_1_ = bf16[8,24,4096]{2,1,0:T(8,128)(2,1)S(1)} collective-permute-done((bf16[8,24,4096]{2,1,0:T(8,128)(2,1)S(1)}, bf16[8,24,4096]{2,1,0:T(8,128)(2,1)S(1)}, u32[]{:S(2)}, u32[]{:S(2)}) %collective-permute-start.6) | collective-permute-done | bytes 1572896 | tf_op jit(solution)/shard_map/ppermute | solution.py:19
  95.0 0.0 collective-permute-done.8.refs_2_
  95.0 1.9 collective-permute-start.10
  96.9 2.4 %collective-permute-start.11 = (bf16[8,64,768]{2,1,0:T(8,128)(2,1)S(1)}, bf16[8,64,768]{2,1,0:T(8,128)(2,1)S(1)}, u32[]{:S(2)}, u32[]{:S(2)}) collective-permute-start(bf16[8,64,768]{2,1,0:T(8,128)(2,1)S(1)} %collective-permute-done.7.refs_5_), channel_id=1, source_target_pairs={{0,16},{16,0},{32,48},{48,32},{64,80},{80,64},{96,112},{112,96},{1... | collective-permute-start | bytes 2359304 | tf_op jit(solution)/shard_map/ppermute | solution.py:19
  99.3 2.1 collective-permute-done.11.refs_7_
  101.4 0.0 collective-permute-done.10.refs_3_
  101.4 12.9 %arrange.1 = (bf16[32,24,4096]{2,1,0:T(8,128)(2,1)S(1)}, bf16[32,64,768]{2,1,0:T(8,128)(2,1)S(1)}) custom-call(bf16[8,24,4096]{2,1,0:T(8,128)(2,1)S(1)} %constant_dynamic-update-slice_fusion.refs_0_, bf16[8,24,4096]{2,1,0:T(8,128)(2,1)S(1)} %collective-permute-done.6.refs_1_, bf16[8,24,4096]{2,1,0:T(8,128)(2,1)S(1)} %collective-permute-done.8.refs_2_, ...), custom_call_target="tpu_custom_call" | custom-call | bytes 19922944 | tf_op jit(solution)/shard_map/arrange/pallas_call | solution.py:92
  114.3 0.0 copy-start.4
  114.3 2.6 %copy-done.4 = bf16[32,24,4096]{2,1,0:T(8,128)(2,1)} copy-done((bf16[32,24,4096]{2,1,0:T(8,128)(2,1)}, bf16[32,24,4096]{2,1,0:T(8,128)(2,1)S(1)}, u32[]{:S(2)}) %copy-start.4) | copy-done | bytes 6291480
  117.0 1.7 copy-done.5
  118.7 0.0 all-to-all-done
  118.7 1.2 copy-done.7
  119.9 9.6 %expert.1 = bf16[384,2048]{1,0:T(8,128)(2,1)} custom-call(bf16[384,2048]{1,0:T(8,128)(2,1)} %bitcast.15, bf16[768,4096]{1,0:T(8,128)(2,1)} %bitcast.13, bf16[2048,768]{1,0:T(8,128)(2,1)} %bitcast.14), custom_call_target="tpu_custom_call" | custom-call | flops 3623878656 | bytes 12582912 | tf_op jit(solution)/shard_map/expert/pallas_call | solution.py:180
  129.5 0.0 copy-start.3
  129.5 0.0 copy-start.9
  129.5 11.2 %all-to-all-start.1 = ((bf16[16,24,2048]{2,1,0:T(8,128)(2,1)}), bf16[16,24,2048]{2,1,0:T(8,128)(2,1)S(1)}, u32[]{:S(2)}, u32[]{:S(2)}) async-start(bf16[16,24,2048]{2,1,0:T(8,128)(2,1)} %bitcast.16), calls=%async_computation.1 | async-start | bytes 3145728 | tf_op jit(solution)/shard_map/all_to_all | solution.py:156
  140.7 0.1 copy.7.expert_ref
  140.8 0.1 copy.8.probs_ref
  140.9 74.4 %all-to-all-done.1 = bf16[16,24,2048]{2,1,0:T(8,128)(2,1)S(1)} async-done(((bf16[16,24,2048]{2,1,0:T(8,128)(2,1)}), bf16[16,24,2048]{2,1,0:T(8,128)(2,1)S(1)}, u32[]{:S(2)}, u32[]{:S(2)}) %all-to-all-start.1) | async-done | bytes 1572896 | tf_op jit(solution)/shard_map/all_to_all | solution.py:156
  215.3 1.6 last.1
  (18 shorter events, 0.2 us)
Async XLA Ops:
  0.0 25.7 %collective-permute-start = (bf16[1,24,4096]{2,1,0:T(8,128)(2,1)}, bf16[1,24,4096]{2,1,0:T(8,128)(2,1)S(1)}, u32[]{:S(2)}, u32[]{:S(2)}) collective-permute-start(bf16[1,24,4096]{2,1,0:T(8,128)(2,1)} %param.10), channel_id=1, source_target_pairs={{0,128},{16,144},{32,160},{48,176},{64,192},{80,208},{96,224},{112... | collective-permute-start | bytes 589832 | tf_op jit(solution)/shard_map/ppermute | solution.py:19
  3.4 22.3 %collective-permute-start.1 = (bf16[1,64,768]{2,1,0:T(8,128)(2,1)}, bf16[1,64,768]{2,1,0:T(8,128)(2,1)S(1)}, u32[]{:S(2)}, u32[]{:S(2)}) collective-permute-start(bf16[1,64,768]{2,1,0:T(8,128)(2,1)} %param.11), channel_id=1, source_target_pairs={{0,32},{16,48},{32,0},{48,16},{64,96},{80,112},{96,64},{112,80},{1... | collective-permute-start | bytes 294920 | tf_op jit(solution)/shard_map/ppermute | solution.py:19
  6.1 1.0 copy-start
  7.1 0.7 copy-start.1
  7.8 0.7 copy-start.2
  10.4 15.4 %copy-start.6 = (bf16[1,24,4096]{2,1,0:T(8,128)(2,1)S(1)}, bf16[1,24,4096]{2,1,0:T(8,128)(2,1)}, u32[]{:S(2)}) copy-start(bf16[1,24,4096]{2,1,0:T(8,128)(2,1)} %param.10) | copy-start | bytes 589828
  10.4 19.4 %copy-start.8 = (bf16[1,64,768]{2,1,0:T(8,128)(2,1)S(1)}, bf16[1,64,768]{2,1,0:T(8,128)(2,1)}, u32[]{:S(2)}) copy-start(bf16[1,64,768]{2,1,0:T(8,128)(2,1)} %param.11) | copy-start | bytes 294916
  10.4 108.3 %all-to-all-start = ((bf16[16,24,2048]{2,1,0:T(8,128)(2,1)}), bf16[16,24,2048]{2,1,0:T(8,128)(2,1)S(1)}, u32[]{:S(2)}, u32[]{:S(2)}) async-start(bf16[16,24,2048]{2,1,0:T(8,128)(2,1)} %bitcast.3), calls=%async_computation | async-start | bytes 3145728 | tf_op jit(solution)/shard_map/all_to_all | solution.py:156
  25.8 13.1 %collective-permute-start.2 = (bf16[2,24,4096]{2,1,0:T(8,128)(2,1)S(1)}, bf16[2,24,4096]{2,1,0:T(8,128)(2,1)S(1)}, u32[]{:S(2)}, u32[]{:S(2)}) collective-permute-start(bf16[2,24,4096]{2,1,0:T(8,128)(2,1)S(1)} %pad_maximum_fusion.1), channel_id=1, source_target_pairs={{0,384},{16,400},{32,416},{48,432},{64,448},{80,464},{96,480},{112... | collective-permute-start | bytes 1179656 | tf_op jit(solution)/shard_map/ppermute | solution.py:19
  29.8 8.8 %collective-permute-start.3 = (bf16[2,64,768]{2,1,0:T(8,128)(2,1)S(1)}, bf16[2,64,768]{2,1,0:T(8,128)(2,1)S(1)}, u32[]{:S(2)}, u32[]{:S(2)}) collective-permute-start(bf16[2,64,768]{2,1,0:T(8,128)(2,1)S(1)} %pad_maximum_fusion.3), channel_id=1, source_target_pairs={{0,96},{16,112},{32,64},{48,80},{64,32},{80,48},{96,0},{112,16},{1... | collective-permute-start | bytes 589832 | tf_op jit(solution)/shard_map/ppermute | solution.py:19
  39.0 19.4 %collective-permute-start.4 = (bf16[4,24,4096]{2,1,0:T(8,128)(2,1)S(1)}, bf16[4,24,4096]{2,1,0:T(8,128)(2,1)S(1)}, u32[]{:S(2)}, u32[]{:S(2)}) collective-permute-start(bf16[4,24,4096]{2,1,0:T(8,128)(2,1)S(1)} %pad_maximum_fusion), channel_id=1, source_target_pairs={{0,32},{16,48},{32,0},{48,16},{64,96},{80,112},{96,64},{112,80},{1... | collective-permute-start | bytes 2359304 | tf_op jit(solution)/shard_map/ppermute | solution.py:19
  42.3 10.7 %collective-permute-start.5 = (bf16[4,64,768]{2,1,0:T(8,128)(2,1)S(1)}, bf16[4,64,768]{2,1,0:T(8,128)(2,1)S(1)}, u32[]{:S(2)}, u32[]{:S(2)}) collective-permute-start(bf16[4,64,768]{2,1,0:T(8,128)(2,1)S(1)} %pad_maximum_fusion.2), channel_id=1, source_target_pairs={{0,128},{16,144},{32,160},{48,176},{64,192},{80,208},{96,224},{112... | collective-permute-start | bytes 1179656 | tf_op jit(solution)/shard_map/ppermute | solution.py:19
  58.5 36.6 %collective-permute-start.6 = (bf16[8,24,4096]{2,1,0:T(8,128)(2,1)S(1)}, bf16[8,24,4096]{2,1,0:T(8,128)(2,1)S(1)}, u32[]{:S(2)}, u32[]{:S(2)}) collective-permute-start(bf16[8,24,4096]{2,1,0:T(8,128)(2,1)S(1)} %constant_dynamic-update-slice_fusion.refs_0_), channel_id=1, source_target_pairs={{0,96},{16,112},{32,64},{48,80},{64,32},{80,48},{96,0},{112,16},{1... | collective-permute-start | bytes 4718600 | tf_op jit(solution)/shard_map/ppermute | solution.py:19
  61.4 33.6 %collective-permute-start.8 = (bf16[8,24,4096]{2,1,0:T(8,128)(2,1)S(1)}, bf16[8,24,4096]{2,1,0:T(8,128)(2,1)S(1)}, u32[]{:S(2)}, u32[]{:S(2)}) collective-permute-start(bf16[8,24,4096]{2,1,0:T(8,128)(2,1)S(1)} %constant_dynamic-update-slice_fusion.refs_0_), channel_id=1, source_target_pairs={{0,16},{16,0},{32,48},{48,32},{64,80},{80,64},{96,112},{112,96},{1... | collective-permute-start | bytes 4718600 | tf_op jit(solution)/shard_map/ppermute | solution.py:19
  63.4 23.0 %collective-permute-start.7 = (bf16[8,64,768]{2,1,0:T(8,128)(2,1)S(1)}, bf16[8,64,768]{2,1,0:T(8,128)(2,1)S(1)}, u32[]{:S(2)}, u32[]{:S(2)}) collective-permute-start(bf16[8,64,768]{2,1,0:T(8,128)(2,1)S(1)} %constant_dynamic-update-slice_fusion.4.refs_4_), channel_id=1, source_target_pairs={{0,384},{16,400},{32,416},{48,432},{64,448},{80,464},{96,480},{112... | collective-permute-start | bytes 2359304 | tf_op jit(solution)/shard_map/ppermute | solution.py:19
  67.4 19.0 %collective-permute-start.9 = (bf16[8,64,768]{2,1,0:T(8,128)(2,1)S(1)}, bf16[8,64,768]{2,1,0:T(8,128)(2,1)S(1)}, u32[]{:S(2)}, u32[]{:S(2)}) collective-permute-start(bf16[8,64,768]{2,1,0:T(8,128)(2,1)S(1)} %constant_dynamic-update-slice_fusion.4.refs_4_), channel_id=1, source_target_pairs={{0,16},{16,0},{32,48},{48,32},{64,80},{80,64},{96,112},{112,96},{1... | collective-permute-start | bytes 2359304 | tf_op jit(solution)/shard_map/ppermute | solution.py:19
  95.0 6.4 %collective-permute-start.10 = (bf16[8,24,4096]{2,1,0:T(8,128)(2,1)S(1)}, bf16[8,24,4096]{2,1,0:T(8,128)(2,1)S(1)}, u32[]{:S(2)}, u32[]{:S(2)}) collective-permute-start(bf16[8,24,4096]{2,1,0:T(8,128)(2,1)S(1)} %collective-permute-done.6.refs_1_), channel_id=1, source_target_pairs={{0,16},{16,0},{32,48},{48,32},{64,80},{80,64},{96,112},{112,96},{1... | collective-permute-start | bytes 4718600 | tf_op jit(solution)/shard_map/ppermute | solution.py:19
  96.9 4.5 %collective-permute-start.11 = (bf16[8,64,768]{2,1,0:T(8,128)(2,1)S(1)}, bf16[8,64,768]{2,1,0:T(8,128)(2,1)S(1)}, u32[]{:S(2)}, u32[]{:S(2)}) collective-permute-start(bf16[8,64,768]{2,1,0:T(8,128)(2,1)S(1)} %collective-permute-done.7.refs_5_), channel_id=1, source_target_pairs={{0,16},{16,0},{32,48},{48,32},{64,80},{80,64},{96,112},{112,96},{1... | collective-permute-start | bytes 2359304 | tf_op jit(solution)/shard_map/ppermute | solution.py:19
  114.3 2.7 %copy-start.4 = (bf16[32,24,4096]{2,1,0:T(8,128)(2,1)}, bf16[32,24,4096]{2,1,0:T(8,128)(2,1)S(1)}, u32[]{:S(2)}) copy-start(bf16[32,24,4096]{2,1,0:T(8,128)(2,1)S(1)} %get-tuple-element.27) | copy-start | bytes 18874372
  117.0 1.7 copy-start.5
  118.7 1.2 copy-start.7
  129.5 11.2 %copy-start.3 = (s32[128]{0:T(128)S(1)}, s32[128]{0:T(128)}, u32[]{:S(2)}) copy-start(s32[128]{0:T(128)} %param.9) | copy-start | bytes 1540
  129.5 11.3 %copy-start.9 = (f32[128,8]{0,1:T(8,128)S(1)}, f32[128,8]{0,1:T(8,128)}, u32[]{:S(2)}) copy-start(f32[128,8]{0,1:T(8,128)} %param.8) | copy-start | bytes 12292
  129.5 85.8 %all-to-all-start.1 = ((bf16[16,24,2048]{2,1,0:T(8,128)(2,1)}), bf16[16,24,2048]{2,1,0:T(8,128)(2,1)S(1)}, u32[]{:S(2)}, u32[]{:S(2)}) async-start(bf16[16,24,2048]{2,1,0:T(8,128)(2,1)} %bitcast.16), calls=%async_computation.1 | async-start | bytes 3145728 | tf_op jit(solution)/shard_map/all_to_all | solution.py:156
